TPU v7x, 32 devices: a whole 2x2x4 slice. The times are simulated.
32 devices in a mesh: fsdp: 32 (over z, y, x, core).
Axes of the slice: x: 2, y: 2, z: 4, core: 2. Of those that a mesh axis runs over, the one named last changes fastest.
Arguments:
- tokens: bfloat16 [4096, 1024], P('fsdp'), may hold values from -6 to 6
- cotangent: bfloat16 [4096, 1024], P('fsdp'), may hold values from -6 to 6
- seq_len: int32 [128], P('fsdp'), may hold values from 0 to 128, as said below
- gain_one: bfloat16 [1024], P('fsdp'), may hold values from 0.5 to 1.5
- w_qkv: bfloat16 [1024, 3072], P('fsdp'), may hold values from -0.1875 to 0.1875
- w_out: bfloat16 [1024, 1024], P('fsdp'), may hold values from -0.5 to 0.5
- gain_two: bfloat16 [1024], P('fsdp'), may hold values from 0.5 to 1.5
- w_in: bfloat16 [1024, 5248], P('fsdp'), may hold values from -0.1875 to 0.1875
- w_down: bfloat16 [1024, 2624], P('fsdp'), may hold values from -0.125 to 0.125
- m_gain_one: float32 [1024], P('fsdp'), may hold values from -40 to 40
- v_gain_one: float32 [1024], P('fsdp'), may hold values from 0.6144 to 6.144
- m_qkv: float32 [1024, 3072], P('fsdp'), may hold values from -40 to 40
- v_qkv: float32 [1024, 3072], P('fsdp'), may hold values from 0.6144 to 6.144
- m_out: float32 [1024, 1024], P('fsdp'), may hold values from -20 to 20
- v_out: float32 [1024, 1024], P('fsdp'), may hold values from 0.16384 to 1.6384
- m_gain_two: float32 [1024], P('fsdp'), may hold values from -40 to 40
- v_gain_two: float32 [1024], P('fsdp'), may hold values from 0.6144 to 6.144
- m_in: float32 [1024, 5248], P('fsdp'), may hold values from -16 to 16
- v_in: float32 [1024, 5248], P('fsdp'), may hold values from 0.11186 to 1.1186
- m_down: float32 [1024, 2624], P('fsdp'), may hold values from -32 to 32
- v_down: float32 [1024, 2624], P('fsdp'), may hold values from 0.32768 to 3.2768
Outputs:
- output: bfloat16 [4096, 1024], P('fsdp')
- grad_tokens: float32 [4096, 1024], P('fsdp')
- grad_gain_one: float32 [1024], P('fsdp')
- grad_qkv: float32 [1024, 3072], P('fsdp')
- grad_out: float32 [1024, 1024], P('fsdp')
- grad_gain_two: float32 [1024], P('fsdp')
- grad_in: float32 [1024, 5248], P('fsdp')
- grad_down: float32 [1024, 2624], P('fsdp')
- new_gain_one: float32 [1024], P('fsdp')
- new_qkv: float32 [1024, 3072], P('fsdp')
- new_out: float32 [1024, 1024], P('fsdp')
- new_gain_two: float32 [1024], P('fsdp')
- new_in: float32 [1024, 5248], P('fsdp')
- new_down: float32 [1024, 2624], P('fsdp')
- new_m_gain_one: float32 [1024], P('fsdp')
- new_v_gain_one: float32 [1024], P('fsdp')
- new_m_qkv: float32 [1024, 3072], P('fsdp')
- new_v_qkv: float32 [1024, 3072], P('fsdp')
- new_m_out: float32 [1024, 1024], P('fsdp')
- new_v_out: float32 [1024, 1024], P('fsdp')
- new_m_gain_two: float32 [1024], P('fsdp')
- new_v_gain_two: float32 [1024], P('fsdp')
- new_m_in: float32 [1024, 5248], P('fsdp')
- new_v_in: float32 [1024, 5248], P('fsdp')
- new_m_down: float32 [1024, 2624], P('fsdp')
- new_v_down: float32 [1024, 2624], P('fsdp')
Inputs may be any that keep to these rules, and one draw needn't show every extreme that they name: `seq_len`: A slot of length 0 holds no sequence; the lengths of one device never add up to more than 128; some slot holds a sequence of 128 tokens.
All inputs are finite; a program needn't handle non-finite values.
Results may differ from a plain program's by a relative error of at most 0.014.
Values may be sent and summed in bfloat16 or wider, within the bound.
A program may use at most 256 MiB of HBM per device.

v0:
```python
from functools import partial
import math
import jax
import jax.numpy as jnp
from jax import lax
from jax.sharding import PartitionSpec as P

HD = 64
STEP = 4
eps_norm = 1e-05
eps_adam = 1e-08
rope_base = 160000.0
beta_one = 0.9
beta_two = 0.999
rate_matrix = 0.01
rate_gain = 0.1
decay_matrix = 0.1
score_scale = 0.125
masked_score = -1e30


def placing(lengths, rows):
    ends = jnp.cumsum(lengths, dtype=jnp.int32)
    starts = ends - lengths
    places = jnp.arange(rows, dtype=jnp.int32)
    inside = ((places[None, :] >= starts[:, None]) & (places[None, :] < ends[:, None])).astype(
        jnp.int32
    )
    slots = jnp.arange(lengths.shape[0], dtype=jnp.int32)
    valid = jnp.sum(inside, axis=0, dtype=jnp.int32)
    segment = (
        jnp.sum(inside * slots[:, None], axis=0, dtype=jnp.int32) + (1 - valid) * lengths.shape[0]
    )
    position = places - jnp.sum(inside * starts[:, None], axis=0, dtype=jnp.int32)
    return (segment, position, valid)


def rope_tables(position):
    exponent = jnp.arange(HD // 2, dtype=jnp.float32) * (-2.0 / HD)
    inverse = jnp.exp(exponent * math.log(rope_base))
    angles = position.astype(jnp.float32)[:, None] * inverse[None, :]
    return (jnp.cos(angles), jnp.sin(angles))


def rotate(tensor, rot_cos, rot_sin):
    half = tensor.shape[-1] // 2
    first = tensor[..., :half]
    second = tensor[..., half:]
    cosine = rot_cos[:, None, :]
    sinus = rot_sin[:, None, :]
    return jnp.concatenate(
        [first * cosine - second * sinus, second * cosine + first * sinus], axis=-1
    )


def unrotate(tensor, rot_cos, rot_sin):
    half = tensor.shape[-1] // 2
    first = tensor[..., :half]
    second = tensor[..., half:]
    cosine = rot_cos[:, None, :]
    sinus = rot_sin[:, None, :]
    return jnp.concatenate(
        [first * cosine + second * sinus, second * cosine - first * sinus], axis=-1
    )


def norm_forward(values_in):
    centre = jnp.mean(values_in, axis=-1, keepdims=True)
    centred = values_in - centre
    inv_std = lax.rsqrt(jnp.mean(centred * centred, axis=-1, keepdims=True) + eps_norm)
    return (centred * inv_std, inv_std)


def norm_input_grad(grad_out, normed, inv_std, gain_f):
    scaled = grad_out * gain_f[None, :]
    first_mean = jnp.mean(scaled, axis=-1, keepdims=True)
    second_mean = jnp.mean(scaled * normed, axis=-1, keepdims=True)
    return inv_std * (scaled - first_mean - normed * second_mean)


def rows_product(left, right):
    return lax.dot_general(
        left, right, (((0,), (0,)), ((), ())), preferred_element_type=jnp.float32
    )


def back_product(left, right):
    return lax.dot_general(
        left, right, (((1,), (1,)), ((), ())), preferred_element_type=jnp.float32
    )


def allowed_pairs(segment):
    return (segment[:, None] == segment[None, :])[None, :, :]


def attend_forward(queries, keys, values, segment):
    scores = (
        jnp.einsum("rhd,shd->hrs", queries, keys, preferred_element_type=jnp.float32) * score_scale
    )
    scores = jnp.where(allowed_pairs(segment), scores, masked_score)
    row_max = jnp.max(scores, axis=-1, keepdims=True)
    row_sum = jnp.sum(jnp.exp(scores - row_max), axis=-1, keepdims=True)
    log_total = row_max + jnp.log(row_sum)
    probs = jnp.exp(scores - log_total).astype(jnp.bfloat16)
    attended = jnp.einsum("hrs,shd->rhd", probs, values, preferred_element_type=jnp.float32)
    return (attended.astype(jnp.bfloat16), log_total)


def attend_backward(queries, keys, values, segment, attended, log_total, grad_att):
    scores = (
        jnp.einsum("rhd,shd->hrs", queries, keys, preferred_element_type=jnp.float32) * score_scale
    )
    scores = jnp.where(allowed_pairs(segment), scores, masked_score)
    probs = jnp.exp(scores - log_total)
    probs_b = probs.astype(jnp.bfloat16)
    grad_values = jnp.einsum("hrs,rhd->shd", probs_b, grad_att, preferred_element_type=jnp.float32)
    grad_probs = jnp.einsum("rhd,shd->hrs", grad_att, values, preferred_element_type=jnp.float32)
    delta = jnp.transpose(
        jnp.sum(grad_att.astype(jnp.float32) * attended.astype(jnp.float32), axis=-1)
    )[:, :, None]
    grad_scores = (probs * (grad_probs - delta) * score_scale).astype(jnp.bfloat16)
    grad_queries = jnp.einsum("hrs,shd->rhd", grad_scores, keys, preferred_element_type=jnp.float32)
    grad_keys = jnp.einsum("hrs,rhd->shd", grad_scores, queries, preferred_element_type=jnp.float32)
    return (grad_queries, grad_keys, grad_values)


def forward_pass(tokens, lengths, weights):
    gain_one, w_qkv, w_out, gain_two, w_in, w_down = weights
    groups = lengths.shape[0]
    rows = tokens.shape[0]
    per_dev = rows // groups
    width = tokens.shape[1]
    heads = width // HD
    ffw = w_in.shape[1] // 2
    segment, position, valid = jax.vmap(partial(placing, rows=per_dev))(lengths)
    rot_cos, rot_sin = rope_tables(position.reshape(rows))
    base = tokens.astype(jnp.float32)
    normed_one, inv_one = norm_forward(base)
    hidden_one = (normed_one * gain_one.astype(jnp.float32)[None, :]).astype(jnp.bfloat16)
    projected = jnp.dot(hidden_one, w_qkv, preferred_element_type=jnp.float32).reshape(
        rows, 3, heads, HD
    )
    queries = rotate(projected[:, 0], rot_cos, rot_sin).astype(jnp.bfloat16)
    keys = rotate(projected[:, 1], rot_cos, rot_sin).astype(jnp.bfloat16)
    values = projected[:, 2].astype(jnp.bfloat16)
    shape_four = (groups, per_dev, heads, HD)
    attended, log_total = jax.vmap(attend_forward)(
        queries.reshape(shape_four), keys.reshape(shape_four), values.reshape(shape_four), segment
    )
    attended_flat = attended.reshape(rows, width)
    residual = base + jnp.dot(attended_flat, w_out, preferred_element_type=jnp.float32)
    normed_two, inv_two = norm_forward(residual)
    hidden_two = (normed_two * gain_two.astype(jnp.float32)[None, :]).astype(jnp.bfloat16)
    lifted = jnp.dot(hidden_two, w_in, preferred_element_type=jnp.float32)
    inner = lifted[:, :ffw]
    gate_part = lifted[:, ffw:]
    cdf = 0.5 * (1.0 + jax.scipy.special.erf(inner * (1.0 / math.sqrt(2.0))))
    activated = inner * cdf
    mixed = (activated * gate_part).astype(jnp.bfloat16)
    output = (residual + back_product(mixed, w_down)).astype(jnp.bfloat16)
    saved = {
        "valid": valid.reshape(rows),
        "segment": segment,
        "rot_cos": rot_cos,
        "rot_sin": rot_sin,
        "normed_one": normed_one,
        "inv_one": inv_one,
        "hidden_one": hidden_one,
        "queries": queries.reshape(shape_four),
        "keys": keys.reshape(shape_four),
        "values": values.reshape(shape_four),
        "attended": attended,
        "log_total": log_total,
        "attended_flat": attended_flat,
        "normed_two": normed_two,
        "inv_two": inv_two,
        "hidden_two": hidden_two,
        "inner": inner,
        "gate_part": gate_part,
        "cdf": cdf,
        "activated": activated,
        "mixed": mixed,
    }
    return (output, saved)


def backward_mlp(cotangent, saved, weights):
    gain_one, w_qkv, w_out, gain_two, w_in, w_down = weights
    grad_rows = cotangent.astype(jnp.float32) * saved["valid"].astype(jnp.float32)[:, None]
    grad_rows_b = grad_rows.astype(jnp.bfloat16)
    grad_mixed = jnp.dot(grad_rows_b, w_down, preferred_element_type=jnp.float32)
    inner = saved["inner"]
    density = jnp.exp(-0.5 * inner * inner) * (1.0 / math.sqrt(2.0 * math.pi))
    grad_inner = grad_mixed * saved["gate_part"] * (saved["cdf"] + inner * density)
    grad_gate = grad_mixed * saved["activated"]
    grad_lift = jnp.concatenate([grad_inner, grad_gate], axis=1).astype(jnp.bfloat16)
    grad_hidden_two = back_product(grad_lift, w_in)
    grad_norm_two = norm_input_grad(
        grad_hidden_two, saved["normed_two"], saved["inv_two"], gain_two.astype(jnp.float32)
    )
    grad_resid = grad_rows + grad_norm_two
    return (grad_resid, (grad_rows_b, grad_lift, grad_hidden_two))


def backward_attention(grad_resid, saved, weights):
    gain_one, w_qkv, w_out, gain_two, w_in, w_down = weights
    shape_four = saved["queries"].shape
    rows = grad_resid.shape[0]
    width = grad_resid.shape[1]
    grad_resid_b = grad_resid.astype(jnp.bfloat16)
    grad_att = back_product(grad_resid_b, w_out).astype(jnp.bfloat16).reshape(shape_four)
    grad_queries, grad_keys, grad_values = jax.vmap(attend_backward)(
        saved["queries"],
        saved["keys"],
        saved["values"],
        saved["segment"],
        saved["attended"],
        saved["log_total"],
        grad_att,
    )
    three_shape = (rows, shape_four[2], shape_four[3])
    grad_queries = unrotate(grad_queries.reshape(three_shape), saved["rot_cos"], saved["rot_sin"])
    grad_keys = unrotate(grad_keys.reshape(three_shape), saved["rot_cos"], saved["rot_sin"])
    grad_values = grad_values.reshape(three_shape)
    grad_proj = (
        jnp.stack([grad_queries, grad_keys, grad_values], axis=1)
        .reshape(rows, 3 * width)
        .astype(jnp.bfloat16)
    )
    grad_hidden_one = back_product(grad_proj, w_qkv)
    grad_norm_one = norm_input_grad(
        grad_hidden_one, saved["normed_one"], saved["inv_one"], gain_one.astype(jnp.float32)
    )
    grad_tokens = grad_resid + grad_norm_one
    return (grad_tokens, (grad_resid_b, grad_proj, grad_hidden_one))


def attention_terms(saved, factors):
    grad_resid_b, grad_proj, grad_hidden_one = factors

    def columns(array):
        return array

    part_qkv = rows_product(columns(saved["hidden_one"]), grad_proj)
    part_out = rows_product(columns(saved["attended_flat"]), grad_resid_b)
    part_one = jnp.sum(columns(grad_hidden_one) * columns(saved["normed_one"]), axis=0)[:, None]
    return jnp.concatenate([part_qkv, part_out, part_one], axis=1)


def mlp_terms(saved, factors):
    grad_rows_b, grad_lift, grad_hidden_two = factors

    def columns(array):
        return array

    part_in = rows_product(columns(saved["hidden_two"]), grad_lift)
    part_down = rows_product(columns(grad_rows_b), saved["mixed"])
    part_two = jnp.sum(columns(grad_hidden_two) * columns(saved["normed_two"]), axis=0)[:, None]
    return jnp.concatenate([part_in, part_down, part_two], axis=1)


def adamw(weight, gradient, first, second, count, rate, decay):
    first_new = beta_one * first + (1.0 - beta_one) * gradient
    second_new = beta_two * second + (1.0 - beta_two) * gradient * gradient
    correct_one = 1.0 - jnp.power(beta_one, count)
    correct_two = 1.0 - jnp.power(beta_two, count)
    weight_f = weight.astype(jnp.float32)
    update = (
        first_new / correct_one / (jnp.sqrt(second_new / correct_two) + eps_adam) + decay * weight_f
    )
    return (weight_f - rate * update, first_new, second_new)


def local(
    tokens,
    cotangent,
    seq_len,
    gain_one,
    w_qkv,
    w_out,
    gain_two,
    w_in,
    w_down,
    m_gain_one,
    v_gain_one,
    m_qkv,
    v_qkv,
    m_out,
    v_out,
    m_gain_two,
    v_gain_two,
    m_in,
    v_in,
    m_down,
    v_down,
):
    gathered = (
        lax.all_gather(gain_one, "fsdp", axis=0, tiled=True),
        lax.all_gather(w_qkv, "fsdp", axis=0, tiled=True),
        lax.all_gather(w_out, "fsdp", axis=0, tiled=True),
        lax.all_gather(gain_two, "fsdp", axis=0, tiled=True),
        lax.all_gather(w_in, "fsdp", axis=0, tiled=True),
        lax.all_gather(w_down, "fsdp", axis=0, tiled=True),
    )
    output, saved = forward_pass(tokens, seq_len.reshape(1, -1), gathered)
    width = tokens.shape[1]
    ffw = w_down.shape[1]
    grad_resid, mlp_factors = backward_mlp(cotangent, saved, gathered)
    mlp_full = mlp_terms(saved, mlp_factors)
    mlp_summed = lax.psum_scatter(mlp_full, "fsdp", scatter_dimension=0, tiled=True)
    grad_tokens, att_factors = backward_attention(grad_resid, saved, gathered)
    att_full = attention_terms(saved, att_factors)
    att_summed = lax.psum_scatter(att_full, "fsdp", scatter_dimension=0, tiled=True)
    shards = (
        att_summed[:, 4 * width],
        att_summed[:, : 3 * width],
        att_summed[:, 3 * width : 4 * width],
        mlp_summed[:, 3 * ffw],
        mlp_summed[:, : 2 * ffw],
        mlp_summed[:, 2 * ffw : 3 * ffw],
    )
    count = jnp.asarray(STEP, jnp.float32)
    weights = (gain_one, w_qkv, w_out, gain_two, w_in, w_down)
    firsts = (m_gain_one, m_qkv, m_out, m_gain_two, m_in, m_down)
    seconds = (v_gain_one, v_qkv, v_out, v_gain_two, v_in, v_down)
    rates = (rate_gain, rate_matrix, rate_matrix, rate_gain, rate_matrix, rate_matrix)
    decays = (0.0, decay_matrix, decay_matrix, 0.0, decay_matrix, decay_matrix)
    results = [
        adamw(weights[i], shards[i], firsts[i], seconds[i], count, rates[i], decays[i])
        for i in range(6)
    ]
    return (
        output,
        grad_tokens,
        shards[0],
        shards[1],
        shards[2],
        shards[3],
        shards[4],
        shards[5],
        results[0][0],
        results[1][0],
        results[2][0],
        results[3][0],
        results[4][0],
        results[5][0],
        results[0][1],
        results[0][2],
        results[1][1],
        results[1][2],
        results[2][1],
        results[2][2],
        results[3][1],
        results[3][2],
        results[4][1],
        results[4][2],
        results[5][1],
        results[5][2],
    )


def solution(mesh):
    placed = (
        P("fsdp", None),
        P("fsdp", None),
        P("fsdp"),
        P("fsdp"),
        P("fsdp", None),
        P("fsdp", None),
        P("fsdp"),
        P("fsdp", None),
        P("fsdp", None),
        P("fsdp"),
        P("fsdp"),
        P("fsdp", None),
        P("fsdp", None),
        P("fsdp", None),
        P("fsdp", None),
        P("fsdp"),
        P("fsdp"),
        P("fsdp", None),
        P("fsdp", None),
        P("fsdp", None),
        P("fsdp", None),
    )
    return jax.shard_map(
        local,
        mesh=mesh,
        in_specs=placed,
        out_specs=(
            P("fsdp", None),
            P("fsdp", None),
            P("fsdp"),
            P("fsdp", None),
            P("fsdp", None),
            P("fsdp"),
            P("fsdp", None),
            P("fsdp", None),
            P("fsdp"),
            P("fsdp", None),
            P("fsdp", None),
            P("fsdp"),
            P("fsdp", None),
            P("fsdp", None),
            P("fsdp"),
            P("fsdp"),
            P("fsdp", None),
            P("fsdp", None),
            P("fsdp", None),
            P("fsdp", None),
            P("fsdp"),
            P("fsdp"),
            P("fsdp", None),
            P("fsdp", None),
            P("fsdp", None),
            P("fsdp", None),
        ),
        check_vma=False,
    )
```

profile of v0, /device:TPU:14, one launch (start us, length us, event | category | flops | bytes accessed | tf_op | source)
XLA Modules:
  0.0 902.6 jit_solution(5415518156487180826)
XLA Ops:
  7.3 0.7 all-gather.5.cloned.1.call-update
  8.0 0.7 all-gather.7.cloned.1.call-update
  8.7 0.7 all-gather.9.cloned.1.call-update
  9.5 0.5 all-gather.11.cloned.1.call-update
  10.1 0.8 dynamic-update-slice
  10.9 0.8 dynamic-update-slice.1
  11.8 40.6 %all-reduce.2 = (bf16[1024]{0:T(1024)(128)(2,1)S(1)}, bf16[1024]{0:T(1024)(128)(2,1)S(1)}) all-reduce(bf16[1024]{0:T(1024)(128)(2,1)S(1)} %dynamic-update-slice, bf16[1024]{0:T(1024)(128)(2,1)S(1)} %dynamic-update-slice.1), channel_id=1, replica_groups=mesh['fsdp'=32] {'fsdp'}, use_global_device_ids=true, to_apply=%add | all-reduce | flops 2048 | bytes 8192
  52.4 0.8 reduce-window.7
  53.2 0.7 bitcast_subtract_fusion
  54.0 1.1 convert_reduce_fusion
  55.0 1.2 fusion.30
  56.2 0.5 fusion.72
  57.0 23.2 %all-gather.5.cloned.1.call-done = bf16[1024,3072]{1,0:T(8,128)(2,1)} async-done(((bf16[32,3072]{1,0:T(8,128)(2,1)}), bf16[1024,3072]{1,0:T(8,128)(2,1)}) %all-gather.5.cloned.1.call-update) | async-done | bytes 6291472 | tf_op jit(solution)/shard_map/all_gather | solution.py:300
  80.3 5.4 fusion.63
  85.8 0.1 subtract_convert_fusion.3
  86.0 0.6 copy-done.18
  86.6 0.4 fusion.73
  87.0 0.2 exponential_reduce_fusion
  87.2 1.0 convolution_convert_fusion.2
  88.2 49.0 %all-gather.7.cloned.1.call-done = bf16[1024,1024]{1,0:T(8,128)(2,1)} async-done(((bf16[32,1024]{1,0:T(8,128)(2,1)}), bf16[1024,1024]{1,0:T(8,128)(2,1)}) %all-gather.7.cloned.1.call-update) | async-done | bytes 2097168 | tf_op jit(solution)/shard_map/all_gather | solution.py:301
  137.1 2.2 fusion.74
  139.4 0.5 copy-done.35
  139.9 0.2 multiply_reduce_fusion.3
  140.1 0.5 add_rsqrt_fusion
  140.6 86.3 %all-gather.9.cloned.1.call-done = bf16[1024,5248]{1,0:T(8,128)(2,1)} async-done(((bf16[32,5248]{1,0:T(8,128)(2,1)}), bf16[1024,5248]{1,0:T(8,128)(2,1)}) %all-gather.9.cloned.1.call-update) | async-done | bytes 10747920 | tf_op jit(solution)/shard_map/all_gather | solution.py:303
  226.9 7.3 fusion.65
  234.2 60.8 %all-gather.11.cloned.1.call-done = bf16[1024,2624]{1,0:T(8,128)(2,1)} async-done(((bf16[32,2624]{1,0:T(8,128)(2,1)}), bf16[1024,2624]{1,0:T(8,128)(2,1)}) %all-gather.11.cloned.1.call-update) | async-done | bytes 5373968 | tf_op jit(solution)/shard_map/all_gather | solution.py:304
  295.0 4.9 fusion.5
  299.9 8.8 multiply_reduce_fusion
  308.8 0.2 multiply_add_fusion.1
  309.1 0.8 copy-done.2
  309.8 1.5 convolution_convert_fusion.1
  311.4 1.8 copy.80
  313.2 1.9 copy.81
  315.1 1.5 fusion.11
  316.7 0.4 fusion.9
  317.2 0.3 copy-done.21
  317.6 0.3 convolution_bitcast_fusion.1
  317.8 0.5 convolution_bitcast_fusion
  318.3 0.3 copy-done.3
  318.6 2.9 fusion.44
  321.5 0.1 add_convert_fusion.1
  321.8 0.5 copy-done.39
  322.3 6.5 fusion.61
  328.8 2.4 fusion.29
  331.1 0.2 copy.87
  331.4 11.5 %pad_maximum_fusion = f32[1024,4097]{1,0:T(8,128)} fusion(f32[1024,1]{1,0:T(8,128)S(1)} %copy.87, f32[1024,1024]{1,0:T(8,128)} %fusion.44, f32[1024,3072]{1,0:T(8,128)} %fusion.61), kind=kLoop, calls=%fused_computation | loop fusion | flops 8390656 | bytes 33562624 | tf_op jit(solution)/shard_map/concatenate | solution.py:248
  343.0 0.6 copy-done.46
  343.6 0.2 copy.89
  343.9 8.2 fusion.47
  352.1 10.5 %fusion.13 = f32[1024,5248]{1,0:T(8,128)} fusion(bf16[128,2624]{1,0:T(8,128)(2,1)S(1)} %copy-done.14, bf16[128,2624]{1,0:T(8,128)(2,1)S(1)} %copy-done.12, f32[128,1024]{1,0:T(8,128)S(1)} %get-tuple-element.82, f32[1024]{0:T(1024)S(1)} %convert_element_type.143, f32[128]{0:T(128)S(1)} %copy-done.41, f32[128]{0:T(128)S(1)} %copy-done.37), kind=kOutput, calls=%fused_computation.32 | convolution fusion | flops 1378942976 | bytes 23368704 | tf_op jit(solution)/shard_map/dot_general | solution.py:82
  362.6 34.4 %concatenate.38 = f32[1024,7873]{1,0:T(8,128)} concatenate(f32[1024,5248]{1,0:T(8,128)} %fusion.13, f32[1024,2624]{1,0:T(8,128)} %fusion.47, f32[1024,1]{1,0:T(8,128)S(1)} %copy.89), dimensions={1} | concatenate | bytes 64495616 | tf_op jit(solution)/shard_map/concatenate | solution.py:260
  397.1 1.0 fusion.28
  398.2 6.9 fusion.10
  405.1 131.9 %reduce-scatter.3.cloned.1.call-done = f32[32,4097]{1,0:T(8,128)} async-done(((f32[1024,4097]{1,0:T(8,128)}), f32[32,4097]{1,0:T(8,128)}) %reduce-scatter.3.cloned.1.call-update) | async-done | bytes 524432 | tf_op jit(solution)/shard_map/reduce_scatter | solution.py:314
  537.1 0.8 slice_reduce_fusion.1
  537.9 0.5 multiply_subtract_fusion.1
  538.5 1.7 convert_subtract_fusion.4
  540.3 2.3 convert_subtract_fusion.2
  542.6 346.7 %reduce-scatter.5.cloned.1.call-done = f32[32,7873]{1,0:T(8,128)} async-done(((f32[1024,7873]{1,0:T(8,128)}), f32[32,7873]{1,0:T(8,128)}) %reduce-scatter.5.cloned.1.call-update) | async-done | bytes 1007760 | tf_op jit(solution)/shard_map/reduce_scatter | solution.py:311
  889.3 0.9 slice_reduce_fusion
  890.2 0.5 multiply_subtract_fusion
  890.8 2.8 convert_subtract_fusion
  893.7 2.1 convert_subtract_fusion.3
  (137 shorter events, 1.3 us)
Async XLA Ops:
  7.2 73.1 %copy-start = (bf16[128,1024]{1,0:T(8,128)(2,1)S(1)}, bf16[128,1024]{1,0:T(8,128)(2,1)}, u32[]{:S(2)}) copy-start(bf16[128,1024]{1,0:T(8,128)(2,1)} %param.21) | copy-start | bytes 786436
  7.2 73.0 %all-gather.5.cloned.1.call-start = ((), (), s32[]{:S(2)}) async-start(), calls=%async_computation.2 | async-start | bytes 6488064 | tf_op jit(solution)/shard_map/all_gather | solution.py:300
  7.9 129.2 %all-gather.7.cloned.1.call-start = ((), (), s32[]{:S(2)}) async-start(), calls=%async_computation.3 | async-start | bytes 2162688 | tf_op jit(solution)/shard_map/all_gather | solution.py:301
  8.7 218.2 %all-gather.9.cloned.1.call-start = ((), (), s32[]{:S(2)}) async-start(), calls=%async_computation.4 | async-start | bytes 11083776 | tf_op jit(solution)/shard_map/all_gather | solution.py:303
  9.4 285.5 %all-gather.11.cloned.1.call-start = ((), (), s32[]{:S(2)}) async-start(), calls=%async_computation.5 | async-start | bytes 5677056 | tf_op jit(solution)/shard_map/all_gather | solution.py:304
  10.0 527.0 %reduce-scatter.3.cloned.1.call-start = ((), (), s32[]{:S(2)}) async-start(), calls=%async_computation.6 | async-start | bytes 17842176 | tf_op jit(solution)/shard_map/reduce_scatter | solution.py:314
  55.0 30.6 %copy-start.38 = (f32[128]{0:T(128)}, f32[128]{0:T(128)S(1)}, u32[]{:S(2)}) copy-start(f32[128]{0:T(128)S(1)} %broadcast_multiply_fusion.5) | copy-start | bytes 1540
  56.2 29.4 %copy-start.42 = (f32[128]{0:T(128)}, f32[128]{0:T(128)S(1)}, u32[]{:S(2)}) copy-start(f32[128]{0:T(128)S(1)} %add_rsqrt_fusion.1) | copy-start | bytes 1540
  57.0 28.8 %copy-start.29 = (f32[128,32]{0,1:T(8,128)}, f32[128,32]{0,1:T(8,128)S(1)}, u32[]{:S(2)}) copy-start(f32[128,32]{0,1:T(8,128)S(1)} %get-tuple-element.75) | copy-start | bytes 49156
  57.0 28.8 %copy-start.31 = (f32[128,32]{0,1:T(8,128)}, f32[128,32]{0,1:T(8,128)S(1)}, u32[]{:S(2)}) copy-start(f32[128,32]{0,1:T(8,128)S(1)} %get-tuple-element.76) | copy-start | bytes 49156
  85.9 0.7 copy-start.18
  85.9 1.0 copy-start.20
  86.0 1.0 copy-start.22
  139.4 0.5 copy-start.35
  294.9 4.9 copy-start.36
  295.0 4.9 copy-start.40
  299.8 8.9 copy-start.11
  299.9 8.9 copy-start.13
  299.9 8.9 copy-start.8
  299.9 8.9 copy-start.44
  299.9 9.9 %copy-start.1 = (bf16[1024,1024]{1,0:T(8,128)(2,1)S(1)}, bf16[1024,1024]{1,0:T(8,128)(2,1)}, u32[]{:S(2)}) copy-start(bf16[1024,1024]{1,0:T(8,128)(2,1)} %all-gather.7.cloned.1.call-done) | copy-start | bytes 6291460
  309.0 0.8 copy-start.2
  315.0 1.5 copy-start.4
  315.1 1.5 copy-start.6
  315.1 1.6 copy-start.5
  316.6 0.9 copy-start.21
  316.6 1.0 copy-start.23
  316.7 1.1 copy-start.19
  317.6 1.1 copy-start.3
  318.6 2.9 copy-start.30
  318.6 2.9 copy-start.32
  321.6 0.7 copy-start.39
  321.6 0.7 copy-start.43
  321.7 7.1 slice-start
  322.3 6.5 slice-start.1
  342.9 0.7 copy-start.46
  342.9 1.0 copy-start.9
  342.9 1.0 copy-start.45
  342.9 546.4 %reduce-scatter.5.cloned.1.call-start = ((), (), s32[]{:S(2)}) async-start(), calls=%async_computation.7 | async-start | bytes 33521664 | tf_op jit(solution)/shard_map/reduce_scatter | solution.py:311
  343.9 8.2 copy-start.12
  343.9 8.2 copy-start.14
  343.9 8.2 copy-start.37
  343.9 8.2 copy-start.41
  398.1 139.7 %copy-start.49 = (bf16[32]{0:T(256)(128)(2,1)S(1)}, bf16[32]{0:T(256)(128)(2,1)}, u32[]{:S(2)}) copy-start(bf16[32]{0:T(256)(128)(2,1)} %param.24) | copy-start | bytes 196
  398.1 139.7 %copy-start.50 = (f32[32]{0:T(128)S(1)}, f32[32]{0:T(128)}, u32[]{:S(2)}) copy-start(f32[32]{0:T(128)} %param.31) | copy-start | bytes 388
  398.1 139.8 %copy-start.51 = (f32[32]{0:T(128)S(1)}, f32[32]{0:T(128)}, u32[]{:S(2)}) copy-start(f32[32]{0:T(128)} %param.30) | copy-start | bytes 388
  398.1 140.3 %copy-start.28 = (bf16[32,1024]{1,0:T(8,128)(2,1)S(1)}, bf16[32,1024]{1,0:T(8,128)(2,1)}, u32[]{:S(2)}) copy-start(bf16[32,1024]{1,0:T(8,128)(2,1)} %param.26) | copy-start | bytes 196612
  398.1 140.3 %copy-start.33 = (f32[32,1024]{1,0:T(8,128)S(1)}, f32[32,1024]{1,0:T(8,128)}, u32[]{:S(2)}) copy-start(f32[32,1024]{1,0:T(8,128)} %param.35) | copy-start | bytes 393220
  398.2 140.3 %copy-start.34 = (f32[32,1024]{1,0:T(8,128)S(1)}, f32[32,1024]{1,0:T(8,128)}, u32[]{:S(2)}) copy-start(f32[32,1024]{1,0:T(8,128)} %param.34) | copy-start | bytes 393220
  398.2 142.0 %copy-start.10 = (bf16[32,3072]{1,0:T(8,128)(2,1)S(1)}, bf16[32,3072]{1,0:T(8,128)(2,1)}, u32[]{:S(2)}) copy-start(bf16[32,3072]{1,0:T(8,128)(2,1)} %param.25) | copy-start | bytes 589828
  398.2 142.0 %copy-start.24 = (f32[32,3072]{1,0:T(8,128)S(1)}, f32[32,3072]{1,0:T(8,128)}, u32[]{:S(2)}) copy-start(f32[32,3072]{1,0:T(8,128)} %param.33) | copy-start | bytes 1179652
  398.2 142.0 %copy-start.25 = (f32[32,3072]{1,0:T(8,128)S(1)}, f32[32,3072]{1,0:T(8,128)}, u32[]{:S(2)}) copy-start(f32[32,3072]{1,0:T(8,128)} %param.32) | copy-start | bytes 1179652
  537.9 4.7 copy-start.47
  540.2 350.0 %copy-start.52 = (bf16[32]{0:T(256)(128)(2,1)S(1)}, bf16[32]{0:T(256)(128)(2,1)}, u32[]{:S(2)}) copy-start(bf16[32]{0:T(256)(128)(2,1)} %param.27) | copy-start | bytes 196
  540.2 350.0 %copy-start.53 = (f32[32]{0:T(128)S(1)}, f32[32]{0:T(128)}, u32[]{:S(2)}) copy-start(f32[32]{0:T(128)} %param.37) | copy-start | bytes 388
  540.2 350.0 %copy-start.54 = (f32[32]{0:T(128)S(1)}, f32[32]{0:T(128)}, u32[]{:S(2)}) copy-start(f32[32]{0:T(128)} %param.36) | copy-start | bytes 388
  540.2 350.5 %copy-start.7 = (bf16[32,5248]{1,0:T(8,128)(2,1)S(1)}, bf16[32,5248]{1,0:T(8,128)(2,1)}, u32[]{:S(2)}) copy-start(bf16[32,5248]{1,0:T(8,128)(2,1)} %param.28) | copy-start | bytes 1007620
  540.3 350.5 %copy-start.16 = (f32[32,5248]{1,0:T(8,128)S(1)}, f32[32,5248]{1,0:T(8,128)}, u32[]{:S(2)}) copy-start(f32[32,5248]{1,0:T(8,128)} %param.39) | copy-start | bytes 2015236
  540.3 350.5 %copy-start.17 = (f32[32,5248]{1,0:T(8,128)S(1)}, f32[32,5248]{1,0:T(8,128)}, u32[]{:S(2)}) copy-start(f32[32,5248]{1,0:T(8,128)} %param.38) | copy-start | bytes 2015236
  890.2 3.4 copy-start.48
  890.8 2.9 copy-start.15
  890.8 2.8 copy-start.26
  890.8 2.8 copy-start.27
Sparse Core Ops, SparseCore 0:
  10.9 69.3 all-gather.4
  83.1 53.9 all-gather.6
  140.0 86.9 all-gather.8
  229.7 65.2 all-gather.10
  343.1 193.9 reduce-scatter.2
  539.2 350.0 reduce-scatter.4
where the time goes:
time: 904 us; the launch traced here: 903 us
  waiting for transfers between devices  701 us (78%)
  matrix products  71.5 us (8%)
  local copies, waits for them, and re-layouts  46.1 us (5%)
  blocking collectives  40.6 us (4%)
  other arithmetic  28.9 us (3%)
  between operations  14.9 us (2%)
    reduce_scatter x1, waiting for transfers between devices, local(): lax.psum_scatter(mlp_full, 'fsdp', scatter_dimension=0, tiled=True)  347 us
    reduce_scatter x1, waiting for transfers between devices, local(): lax.psum_scatter(att_full, 'fsdp', scatter_dimension=0, tiled=True)  132 us
    all_gather x1, waiting for transfers between devices, local(): lax.all_gather(w_in, 'fsdp', axis=0, tiled=True)  86.3 us
    all_gather x1, waiting for transfers between devices, local(): lax.all_gather(w_down, 'fsdp', axis=0, tiled=True)  60.8 us
    all_gather x1, waiting for transfers between devices, local(): lax.all_gather(w_out, 'fsdp', axis=0, tiled=True)  49 us
    unnamed x1, blocking collectives  40.6 us
    concatenate x1, local copies, waits for them, and re-layouts, mlp_terms(): return jnp.concatenate([part_in, part_down, part_two], axis=1)  34.4 us
    dot_general x4, matrix products, rows_product(): lax.dot_general(left, right, (((0,), (0,)), ((), ())), preferred_element_...  28 us
  transfers between devices with their start and end apart: 6, of which 6 were waited for; matrix products, arithmetic and copies ran while one was open for 10% of the time, Pallas kernels for 0%

commit v1 on v0

--- a/solution.py
+++ b/solution.py
@@ -17,6 +17,18 @@
 decay_matrix = 0.1
 score_scale = 0.125
 masked_score = -1e30
+
+
+def collect(x, axis, dim):
+    ways, here = (lax.axis_size(axis), lax.axis_index(axis))
+    grown, reach = (x, 1)
+    while reach < ways:
+        theirs = lax.ppermute(grown, axis, [(d, d ^ reach) for d in range(ways)])
+        mine_first = jnp.concatenate([grown, theirs], axis=dim)
+        theirs_first = jnp.concatenate([theirs, grown], axis=dim)
+        grown = jnp.where(here & reach == 0, mine_first, theirs_first)
+        reach = 2 * reach
+    return grown
 
 
 def placing(lengths, rows):
@@ -300,7 +312,7 @@
         lax.all_gather(w_qkv, "fsdp", axis=0, tiled=True),
         lax.all_gather(w_out, "fsdp", axis=0, tiled=True),
         lax.all_gather(gain_two, "fsdp", axis=0, tiled=True),
-        lax.all_gather(w_in, "fsdp", axis=0, tiled=True),
+        collect(w_in, "fsdp", 0),
         lax.all_gather(w_down, "fsdp", axis=0, tiled=True),
     )
     output, saved = forward_pass(tokens, seq_len.reshape(1, -1), gathered)

time: 904 us -> 1040 us (1.15)
  blocking collectives: 40.6 us -> 247 us
  waiting for transfers between devices: 701 us -> 612 us
    unnamed x1, blocking collectives: 40.6 us -> 247 us
    ppermute x0 -> x5, waiting for transfers between devices: none -> 130 us  [collect(): theirs = lax.ppermute(grown, axis, [(d, d ^ reach) for d in range(ways)])]
    all_gather x1 -> x0, waiting for transfers between devices: 86.3 us -> none  [local(): lax.all_gather(w_in, 'fsdp', axis=0, tiled=True)]
    all_gather x1, waiting for transfers between devices: 60.8 us -> 3.2 us  [local(): lax.all_gather(w_down, 'fsdp', axis=0, tiled=True)]
    all_gather x1, waiting for transfers between devices: 49 us -> 0.01 us  [local(): lax.all_gather(w_out, 'fsdp', axis=0, tiled=True)]
    all_gather x1, waiting for transfers between devices: 23.2 us -> 0.02 us  [local(): lax.all_gather(w_qkv, 'fsdp', axis=0, tiled=True)]
    select_n x0 -> x4, other arithmetic: none -> 11.3 us  [collect(): grown = jnp.where(here & reach == 0, mine_first, theirs_first)]
  transfers between devices with their start and end apart: 6 -> 10, of which waited for: 6 -> 7; matrix products, arithmetic and copies ran while one was open for 10% -> 10% of each run, Pallas kernels for 0% -> 0%
where the time goes in v1:
time: 1040 us
  waiting for transfers between devices  612 us (59%)
  blocking collectives  247 us (24%)
  matrix products  78.6 us (8%)
  local copies, waits for them, and re-layouts  45 us (4%)
  other arithmetic  39.1 us (4%)
  between operations  14.5 us (1%)
    reduce_scatter x1, waiting for transfers between devices, local(): lax.psum_scatter(mlp_full, 'fsdp', scatter_dimension=0, tiled=True)  347 us
    unnamed x1, blocking collectives  247 us
    reduce_scatter x1, waiting for transfers between devices, local(): lax.psum_scatter(att_full, 'fsdp', scatter_dimension=0, tiled=True)  131 us
    ppermute x5, waiting for transfers between devices, collect(): theirs = lax.ppermute(grown, axis, [(d, d ^ reach) for d in range(ways)])  130 us
    concatenate x1, local copies, waits for them, and re-layouts, mlp_terms(): return jnp.concatenate([part_in, part_down, part_two], axis=1)  34.4 us
    dot_general x4, matrix products, rows_product(): lax.dot_general(left, right, (((0,), (0,)), ((), ())), preferred_element_...  27.9 us
    dot_general x4, matrix products, back_product(): lax.dot_general(left, right, (((1,), (1,)), ((), ())), preferred_element_...  22.5 us
  transfers between devices with their start and end apart: 10, of which 7 were waited for; matrix products, arithmetic and copies ran while one was open for 10% of the time, Pallas kernels for 0%

profile of v1, /device:TPU:14, one launch (start us, length us, event | category | flops | bytes accessed | tf_op | source)
XLA Modules:
  0.0 1042.1 jit_solution(2752671077654930489)
XLA Ops:
  7.2 0.7 all-gather.4.cloned.1.call-update
  8.0 0.7 all-gather.6.cloned.1.call-update
  8.8 1.8 collective-permute-done
  10.6 1.3 maximum_select_fusion.6
  12.0 0.6 collective-permute-start.1
  12.6 18.0 %collective-permute-done.1 = bf16[64,5248]{1,0:T(8,128)(2,1)S(1)} collective-permute-done((bf16[64,5248]{1,0:T(8,128)(2,1)S(1)}, bf16[64,5248]{1,0:T(8,128)(2,1)S(1)}, u32[]{:S(2)}, u32[]{:S(2)}) %collective-permute-start.1) | collective-permute-done | bytes 671776 | tf_op jit(solution)/shard_map/ppermute | solution.py:26
  30.6 0.2 maximum_select_fusion.5
  30.8 0.6 collective-permute-start.2
  31.5 38.3 %collective-permute-done.2 = bf16[128,5248]{1,0:T(8,128)(2,1)S(1)} collective-permute-done((bf16[128,5248]{1,0:T(8,128)(2,1)S(1)}, bf16[128,5248]{1,0:T(8,128)(2,1)S(1)}, u32[]{:S(2)}, u32[]{:S(2)}) %collective-permute-start.2) | collective-permute-done | bytes 1343520 | tf_op jit(solution)/shard_map/ppermute | solution.py:26
  69.7 1.9 maximum_select_fusion.2
  71.7 0.4 collective-permute-start.3
  72.0 71.4 %collective-permute-done.3 = bf16[256,5248]{1,0:T(8,128)(2,1)} collective-permute-done((bf16[256,5248]{1,0:T(8,128)(2,1)}, bf16[256,5248]{1,0:T(8,128)(2,1)}, u32[]{:S(2)}, u32[]{:S(2)}) %collective-permute-start.3) | collective-permute-done | bytes 2687008 | tf_op jit(solution)/shard_map/ppermute | solution.py:26
  143.5 7.8 maximum_select_fusion.1
  151.2 3.9 collective-permute-start.4
  155.3 0.2 dynamic-update-slice.1
  155.6 247.3 %all-reduce.2 = (bf16[1024]{0:T(1024)(128)(2,1)S(1)}, bf16[1024]{0:T(1024)(128)(2,1)S(1)}) all-reduce(bf16[1024]{0:T(1024)(128)(2,1)S(1)} %dynamic-update-slice, bf16[1024]{0:T(1024)(128)(2,1)S(1)} %dynamic-update-slice.1), channel_id=1, replica_groups=mesh['fsdp'=32] {'fsdp'}, use_global_device_ids=true, to_apply=%add | all-reduce | flops 2048 | bytes 8192
  403.3 0.2 fusion.31
  403.5 0.5 fusion.73
  404.0 0.7 broadcast_compare_fusion
  404.9 5.4 fusion.65
  410.6 0.6 copy-done.17
  411.3 0.4 fusion.74
  411.8 1.0 convolution_convert_fusion.2
  412.8 2.3 fusion.75
  415.4 0.3 copy-done.39
  415.6 0.2 copy-done.42
  415.9 10.7 %fusion.1 = f32[128,5248]{1,0:T(8,128)} fusion(bf16[512,5248]{1,0:T(8,128)(2,1)} %collective-permute-done.4, bf16[512,5248]{1,0:T(8,128)(2,1)} %maximum_select_fusion.1, pred[]{:T(512)S(6)} %eq.44, f32[128,1024]{1,0:T(8,128)S(1)} %get-tuple-element.82, f32[1024]{0:T(1024)S(1)} %convert_element_type.143, f32[128]{0:T(128)S(1)} %add_rsqrt_fusion, ...), kind=kOutput, calls=%fused_computation.6 | convolution fusion | flops 1424621568 | bytes 13964289 | tf_op jit(solution)/shard_map/dot_general | solution.py:167
  426.6 3.2 all-gather.8.cloned.1.call-done
  429.8 4.9 fusion.7
  434.8 11.8 %multiply_reduce_fusion = (f32[1024]{0:T(1024)}, f32[128]{0:T(128)S(1)}, f32[128]{0:T(128)S(1)}, f32[128,1024]{1,0:T(8,128)}) fusion(f32[128,1024]{1,0:T(8,128)S(1)} %get-tuple-element.82, f32[128]{0:T(128)S(1)} %copy-done.43, f32[128]{0:T(128)S(1)} %copy-done.40, f32[1024]{0:T(1024)S(1)} %convert_element_type.143, ...), kind=kOutput, calls=%fused_computation.66 | convolution fusion | flops 1427831552 | bytes 13150209 | tf_op jit(solution)/shard_map/dot_general | solution.py:100
  446.6 1.3 multiply_add_fusion.1
  447.9 0.8 copy-done.2
  448.7 1.5 convolution_convert_fusion.1
  450.2 1.8 copy.80
  452.0 1.9 copy.81
  453.9 1.5 fusion.13
  455.4 1.2 multiply_reduce_fusion.1
  456.6 1.4 fusion.11
  458.1 0.3 convolution_bitcast_fusion.1
  458.3 0.4 convolution_bitcast_fusion
  458.8 2.7 fusion.45
  461.8 0.3 copy-done.35
  462.2 6.5 fusion.63
  468.7 2.4 fusion.30
  471.0 0.2 copy.87
  471.2 11.5 %pad_maximum_fusion = f32[1024,4097]{1,0:T(8,128)} fusion(f32[1024,1]{1,0:T(8,128)S(1)} %copy.87, f32[1024,1024]{1,0:T(8,128)} %fusion.45, f32[1024,3072]{1,0:T(8,128)} %fusion.63), kind=kLoop, calls=%fused_computation | loop fusion | flops 8390656 | bytes 33562624 | tf_op jit(solution)/shard_map/concatenate | solution.py:260
  482.9 0.6 copy-done.47
  483.5 0.2 copy.89
  483.8 8.2 fusion.48
  492.0 10.6 %fusion.15 = f32[1024,5248]{1,0:T(8,128)} fusion(bf16[128,2624]{1,0:T(8,128)(2,1)S(1)} %copy-done.13, bf16[128,2624]{1,0:T(8,128)(2,1)S(1)} %copy-done.11, f32[128,1024]{1,0:T(8,128)S(1)} %get-tuple-element.82, f32[1024]{0:T(1024)S(1)} %convert_element_type.143, f32[128]{0:T(128)S(1)} %copy-done.44, f32[128]{0:T(128)S(1)} %copy-done.41), kind=kOutput, calls=%fused_computation.38 | convolution fusion | flops 1378942976 | bytes 23368704 | tf_op jit(solution)/shard_map/dot_general | solution.py:94
  502.6 34.4 %concatenate.78 = f32[1024,7873]{1,0:T(8,128)} concatenate(f32[1024,5248]{1,0:T(8,128)} %fusion.15, f32[1024,2624]{1,0:T(8,128)} %fusion.48, f32[1024,1]{1,0:T(8,128)S(1)} %copy.89), dimensions={1} | concatenate | bytes 64495616 | tf_op jit(solution)/shard_map/concatenate | solution.py:272
  537.0 1.0 copy-done.4
  538.0 1.0 fusion.29
  539.1 6.8 fusion.12
  545.9 131.0 %reduce-scatter.3.cloned.1.call-done = f32[32,4097]{1,0:T(8,128)} async-done(((f32[1024,4097]{1,0:T(8,128)}), f32[32,4097]{1,0:T(8,128)}) %reduce-scatter.3.cloned.1.call-update) | async-done | bytes 524432 | tf_op jit(solution)/shard_map/reduce_scatter | solution.py:326
  677.0 0.8 slice_reduce_fusion.1
  677.8 0.5 multiply_subtract_fusion.1
  678.4 1.7 convert_subtract_fusion.4
  680.1 2.2 convert_subtract_fusion.2
  682.4 346.8 %reduce-scatter.5.cloned.1.call-done = f32[32,7873]{1,0:T(8,128)} async-done(((f32[1024,7873]{1,0:T(8,128)}), f32[32,7873]{1,0:T(8,128)}) %reduce-scatter.5.cloned.1.call-update) | async-done | bytes 1007760 | tf_op jit(solution)/shard_map/reduce_scatter | solution.py:323
  1029.1 0.9 slice_reduce_fusion
  1030.1 0.5 multiply_subtract_fusion
  1030.6 2.8 convert_subtract_fusion
  1033.4 2.1 convert_subtract_fusion.3
  (156 shorter events, 2.4 us)
Async XLA Ops:
  7.2 397.7 %all-gather.4.cloned.1.call-start = ((), (), s32[]{:S(2)}) async-start(), calls=%async_computation.2 | async-start | bytes 6488064 | tf_op jit(solution)/shard_map/all_gather | solution.py:312
  7.9 404.9 %all-gather.6.cloned.1.call-start = ((), (), s32[]{:S(2)}) async-start(), calls=%async_computation.3 | async-start | bytes 2162688 | tf_op jit(solution)/shard_map/all_gather | solution.py:313
  8.7 421.1 %all-gather.8.cloned.1.call-start = ((), (), s32[]{:S(2)}) async-start(), calls=%async_computation.4 | async-start | bytes 5677056 | tf_op jit(solution)/shard_map/all_gather | solution.py:316
  8.7 1.9 collective-permute-start
  12.0 18.6 %collective-permute-start.1 = (bf16[64,5248]{1,0:T(8,128)(2,1)S(1)}, bf16[64,5248]{1,0:T(8,128)(2,1)S(1)}, u32[]{:S(2)}, u32[]{:S(2)}) collective-permute-start(bf16[64,5248]{1,0:T(8,128)(2,1)S(1)} %maximum_select_fusion.6), channel_id=1, source_target_pairs={{0,2},{1,3},{2,0},{3,1},{4,6},{5,7},{6,4},{7,5},{8,10},{9,11},{10,... | collective-permute-start | bytes 2015240 | tf_op jit(solution)/shard_map/ppermute | solution.py:26
  30.8 38.9 %collective-permute-start.2 = (bf16[128,5248]{1,0:T(8,128)(2,1)S(1)}, bf16[128,5248]{1,0:T(8,128)(2,1)S(1)}, u32[]{:S(2)}, u32[]{:S(2)}) collective-permute-start(bf16[128,5248]{1,0:T(8,128)(2,1)S(1)} %maximum_select_fusion.5), channel_id=1, source_target_pairs={{0,4},{1,5},{2,6},{3,7},{4,0},{5,1},{6,2},{7,3},{8,12},{9,13},{10,... | collective-permute-start | bytes 4030472 | tf_op jit(solution)/shard_map/ppermute | solution.py:26
  31.4 645.6 %reduce-scatter.3.cloned.1.call-start = ((), (), s32[]{:S(2)}) async-start(), calls=%async_computation.5 | async-start | bytes 17842176 | tf_op jit(solution)/shard_map/reduce_scatter | solution.py:326
  71.7 71.8 %collective-permute-start.3 = (bf16[256,5248]{1,0:T(8,128)(2,1)}, bf16[256,5248]{1,0:T(8,128)(2,1)}, u32[]{:S(2)}, u32[]{:S(2)}) collective-permute-start(bf16[256,5248]{1,0:T(8,128)(2,1)} %maximum_select_fusion.2), channel_id=1, source_target_pairs={{0,8},{1,9},{2,10},{3,11},{4,12},{5,13},{6,14},{7,15},{8,0},{9,1},... | collective-permute-start | bytes 8060936 | tf_op jit(solution)/shard_map/ppermute | solution.py:26
  72.0 83.1 %copy-start.50 = (bf16[32]{0:T(256)(128)(2,1)S(1)}, bf16[32]{0:T(256)(128)(2,1)}, u32[]{:S(2)}) copy-start(bf16[32]{0:T(256)(128)(2,1)} %param.24) | copy-start | bytes 196
  72.0 83.3 %copy-start.54 = (bf16[32]{0:T(256)(128)(2,1)S(1)}, bf16[32]{0:T(256)(128)(2,1)}, u32[]{:S(2)}) copy-start(bf16[32]{0:T(256)(128)(2,1)} %param.27) | copy-start | bytes 196
  72.0 330.8 %copy-start.58 = (s32[4]{0:T(128)S(1)}, s32[4]{0:T(128)}, u32[]{:S(2)}) copy-start(s32[4]{0:T(128)} %param.23) | copy-start | bytes 52
  72.0 331.1 %copy-start = (bf16[128,1024]{1,0:T(8,128)(2,1)S(1)}, bf16[128,1024]{1,0:T(8,128)(2,1)}, u32[]{:S(2)}) copy-start(bf16[128,1024]{1,0:T(8,128)(2,1)} %param.21) | copy-start | bytes 786436
  151.2 264.1 %collective-permute-start.4 = (bf16[512,5248]{1,0:T(8,128)(2,1)}, bf16[512,5248]{1,0:T(8,128)(2,1)}, u32[]{:S(2)}, u32[]{:S(2)}) collective-permute-start(bf16[512,5248]{1,0:T(8,128)(2,1)} %maximum_select_fusion.1), channel_id=1, source_target_pairs={{0,16},{1,17},{2,18},{3,19},{4,20},{5,21},{6,22},{7,23},{8,24},{9,... | collective-permute-start | bytes 16121864 | tf_op jit(solution)/shard_map/ppermute | solution.py:26
  403.2 7.1 copy-start.34
  403.5 6.8 copy-start.37
  404.9 5.6 copy-start.28
  404.9 5.6 copy-start.30
  410.3 0.9 copy-start.36
  410.6 1.0 copy-start.19
  410.6 1.0 copy-start.21
  429.8 4.9 copy-start.40
  429.8 4.9 copy-start.43
  434.7 11.9 %copy-start.10 = (bf16[128,2624]{1,0:T(8,128)(2,1)}, bf16[128,2624]{1,0:T(8,128)(2,1)S(1)}, u32[]{:S(2)}) copy-start(bf16[128,2624]{1,0:T(8,128)(2,1)S(1)} %get-tuple-element.59) | copy-start | bytes 2015236
  434.7 11.9 %copy-start.12 = (bf16[128,2624]{1,0:T(8,128)(2,1)}, bf16[128,2624]{1,0:T(8,128)(2,1)S(1)}, u32[]{:S(2)}) copy-start(bf16[128,2624]{1,0:T(8,128)(2,1)S(1)} %get-tuple-element.60) | copy-start | bytes 2015236
  434.7 11.9 %copy-start.7 = (bf16[128,1024]{1,0:T(8,128)(2,1)S(1)}, bf16[128,1024]{1,0:T(8,128)(2,1)}, u32[]{:S(2)}) copy-start(bf16[128,1024]{1,0:T(8,128)(2,1)} %param.22) | copy-start | bytes 786436
  434.7 11.9 %copy-start.45 = (f32[128]{0:T(128)S(1)}, f32[128]{0:T(128)}, u32[]{:S(2)}) copy-start(f32[128]{0:T(128)} %get-tuple-element.77) | copy-start | bytes 1540
  434.7 14.0 %copy-start.1 = (bf16[1024,1024]{1,0:T(8,128)(2,1)S(1)}, bf16[1024,1024]{1,0:T(8,128)(2,1)}, u32[]{:S(2)}) copy-start(bf16[1024,1024]{1,0:T(8,128)(2,1)} %all-gather.6.cloned.1.call-done) | copy-start | bytes 6291460
  453.9 4.2 copy-start.20
  453.9 4.2 copy-start.22
  453.9 4.4 copy-start.18
  456.6 2.2 copy-start.3
  456.6 2.2 copy-start.5
  458.8 2.7 copy-start.29
  458.8 2.7 copy-start.31
  461.7 6.9 slice-start
  462.2 6.5 slice-start.1
  482.8 1.0 copy-start.8
  482.8 1.0 copy-start.46
  482.8 546.3 %reduce-scatter.5.cloned.1.call-start = ((), (), s32[]{:S(2)}) async-start(), calls=%async_computation.6 | async-start | bytes 33521664 | tf_op jit(solution)/shard_map/reduce_scatter | solution.py:323
  483.8 8.2 copy-start.11
  483.8 8.2 copy-start.13
  483.8 8.2 copy-start.41
  483.8 8.2 copy-start.44
  537.0 1.0 copy-start.4
  539.1 138.8 %copy-start.51 = (bf16[32]{0:T(256)(128)(2,1)S(1)}, bf16[32]{0:T(256)(128)(2,1)}, u32[]{:S(2)}) copy-start(bf16[32]{0:T(256)(128)(2,1)} %param.24) | copy-start | bytes 196
  539.1 138.8 %copy-start.52 = (f32[32]{0:T(128)S(1)}, f32[32]{0:T(128)}, u32[]{:S(2)}) copy-start(f32[32]{0:T(128)} %param.31) | copy-start | bytes 388
  539.1 138.8 %copy-start.53 = (f32[32]{0:T(128)S(1)}, f32[32]{0:T(128)}, u32[]{:S(2)}) copy-start(f32[32]{0:T(128)} %param.30) | copy-start | bytes 388
  539.1 139.3 %copy-start.27 = (bf16[32,1024]{1,0:T(8,128)(2,1)S(1)}, bf16[32,1024]{1,0:T(8,128)(2,1)}, u32[]{:S(2)}) copy-start(bf16[32,1024]{1,0:T(8,128)(2,1)} %param.26) | copy-start | bytes 196612
  539.1 139.3 %copy-start.32 = (f32[32,1024]{1,0:T(8,128)S(1)}, f32[32,1024]{1,0:T(8,128)}, u32[]{:S(2)}) copy-start(f32[32,1024]{1,0:T(8,128)} %param.35) | copy-start | bytes 393220
  539.1 139.3 %copy-start.33 = (f32[32,1024]{1,0:T(8,128)S(1)}, f32[32,1024]{1,0:T(8,128)}, u32[]{:S(2)}) copy-start(f32[32,1024]{1,0:T(8,128)} %param.34) | copy-start | bytes 393220
  539.1 141.0 %copy-start.9 = (bf16[32,3072]{1,0:T(8,128)(2,1)S(1)}, bf16[32,3072]{1,0:T(8,128)(2,1)}, u32[]{:S(2)}) copy-start(bf16[32,3072]{1,0:T(8,128)(2,1)} %param.25) | copy-start | bytes 589828
  539.1 141.0 %copy-start.23 = (f32[32,3072]{1,0:T(8,128)S(1)}, f32[32,3072]{1,0:T(8,128)}, u32[]{:S(2)}) copy-start(f32[32,3072]{1,0:T(8,128)} %param.33) | copy-start | bytes 1179652
  539.1 141.0 %copy-start.24 = (f32[32,3072]{1,0:T(8,128)S(1)}, f32[32,3072]{1,0:T(8,128)}, u32[]{:S(2)}) copy-start(f32[32,3072]{1,0:T(8,128)} %param.32) | copy-start | bytes 1179652
  545.9 484.1 %copy-start.55 = (bf16[32]{0:T(256)(128)(2,1)S(1)}, bf16[32]{0:T(256)(128)(2,1)}, u32[]{:S(2)}) copy-start(bf16[32]{0:T(256)(128)(2,1)} %param.27) | copy-start | bytes 196
  545.9 484.2 %copy-start.56 = (f32[32]{0:T(128)S(1)}, f32[32]{0:T(128)}, u32[]{:S(2)}) copy-start(f32[32]{0:T(128)} %param.37) | copy-start | bytes 388
  545.9 484.2 %copy-start.57 = (f32[32]{0:T(128)S(1)}, f32[32]{0:T(128)}, u32[]{:S(2)}) copy-start(f32[32]{0:T(128)} %param.36) | copy-start | bytes 388
  545.9 484.7 %copy-start.6 = (bf16[32,5248]{1,0:T(8,128)(2,1)S(1)}, bf16[32,5248]{1,0:T(8,128)(2,1)}, u32[]{:S(2)}) copy-start(bf16[32,5248]{1,0:T(8,128)(2,1)} %param.28) | copy-start | bytes 1007620
  545.9 484.7 %copy-start.15 = (f32[32,5248]{1,0:T(8,128)S(1)}, f32[32,5248]{1,0:T(8,128)}, u32[]{:S(2)}) copy-start(f32[32,5248]{1,0:T(8,128)} %param.39) | copy-start | bytes 2015236
  545.9 484.7 %copy-start.16 = (f32[32,5248]{1,0:T(8,128)S(1)}, f32[32,5248]{1,0:T(8,128)}, u32[]{:S(2)}) copy-start(f32[32,5248]{1,0:T(8,128)} %param.38) | copy-start | bytes 2015236
  677.8 355.6 %copy-start.48 = (f32[32]{0:T(128)}, f32[32]{0:T(128)S(1)}, u32[]{:S(2)}) copy-start(f32[32]{0:T(128)S(1)} %slice_reduce_fusion.1) | copy-start | bytes 388
  682.3 351.1 %copy-start.14 = (bf16[32,2624]{1,0:T(8,128)(2,1)S(1)}, bf16[32,2624]{1,0:T(8,128)(2,1)}, u32[]{:S(2)}) copy-start(bf16[32,2624]{1,0:T(8,128)(2,1)} %param.29) | copy-start | bytes 503812
  682.3 351.1 %copy-start.25 = (f32[32,2624]{1,0:T(8,128)S(1)}, f32[32,2624]{1,0:T(8,128)}, u32[]{:S(2)}) copy-start(f32[32,2624]{1,0:T(8,128)} %param.41) | copy-start | bytes 1007620
  682.4 351.1 %copy-start.26 = (f32[32,2624]{1,0:T(8,128)S(1)}, f32[32,2624]{1,0:T(8,128)}, u32[]{:S(2)}) copy-start(f32[32,2624]{1,0:T(8,128)} %param.40) | copy-start | bytes 1007620
  1030.1 5.5 copy-start.49
  (7 other events, 4.5 us)
Sparse Core Ops, SparseCore 0:
  10.9 80.8 all-gather.3
  94.6 55.7 all-gather.5
  153.3 276.3 all-gather.7
  482.9 193.9 reduce-scatter.2
  679.1 349.9 reduce-scatter.4
